TPU v7x, 128 devices: a whole 4x4x4 slice. The times are simulated.
128 devices in a mesh: smp: 8 (over x_lo, z), bld: 16 (over y, x_hi, core).
Axes of the slice: x: 4 (x_hi: 2, x_lo: 2; x = x_hi * 2 + x_lo), y: 4, z: 4, core: 2. Of those that a mesh axis runs over, the one named last changes fastest.
Arguments:
- tensor: bfloat16 [4, 8192, 16384], P(None, 'smp', 'bld'), may hold values from -576 to 576
- building_factor: float32 [64, 16384], P(None, 'bld'), may hold values from -144 to 144
- hour_weights: float32 [4, 64], replicated, may hold values from -5 to 5
Outputs:
- sample_factor: float32 [64, 8192], P(None, ('smp', 'bld'))
- building_out: float32 [64, 16384], P(None, ('bld', 'smp'))
- hour_out: float32 [4, 64], replicated
All inputs are finite; a program needn't handle non-finite values.
Results may differ from a plain program's by a relative error of at most 0.008.
Values may be sent and summed in bfloat16 or wider, within the bound.
A program may use at most 64 MiB of HBM per device.

v0:
```python
import math
import jax
import jax.numpy as jnp
from jax import lax
from jax.sharding import PartitionSpec as P

SWEEPS = 5
EPSILON = 1e-06
RIDGE_SHARE = 0.05


def regularized(gram):
    order_size = gram.shape[0]
    return gram + RIDGE_SHARE * jnp.mean(jnp.diagonal(gram)) * jnp.eye(order_size, dtype=gram.dtype)


def solve_rows(gram, right_side):
    lower_factor = jnp.linalg.cholesky(regularized(gram))
    middle = lax.linalg.triangular_solve(lower_factor, right_side, left_side=True, lower=True)
    return lax.linalg.triangular_solve(
        lower_factor, middle, left_side=True, lower=True, transpose_a=True
    )


def finish(unscaled, gram_raw, row_count):
    column_norm = jnp.sqrt(jnp.diagonal(gram_raw) / row_count + EPSILON)
    return (
        unscaled / column_norm[:, None],
        gram_raw / (column_norm[:, None] * column_norm[None, :]),
    )


def hour_gram(hourly):
    return jnp.dot(hourly.T, hourly, precision=lax.Precision.HIGHEST)


def self_gram(unscaled):
    return jnp.dot(unscaled, unscaled.T, precision=lax.Precision.HIGHEST)


def local(tensor, building_factor, hour_weights):
    samples_total = tensor.shape[1] * lax.axis_size("smp")
    buildings_total = tensor.shape[2] * lax.axis_size("bld")
    scale_up = math.sqrt(samples_total * buildings_total)
    hourly = hour_weights / scale_up
    gram_build = lax.psum(self_gram(building_factor), "bld")
    build_low = building_factor.astype(jnp.bfloat16)
    partial_value = jnp.einsum("rj,kij->kri", build_low, tensor, preferred_element_type=jnp.float32)
    sample_out = None
    building_out = None
    for sweep_index in range(SWEEPS):
        sample_terms = jnp.sum(hourly[:, :, None] * partial_value, axis=0)
        sample_rhs = lax.psum(sample_terms, "bld")
        unscaled = solve_rows(gram_build * hour_gram(hourly), sample_rhs)
        gram_raw = lax.psum(self_gram(unscaled), "smp")
        samples_now, gram_sample = finish(unscaled, gram_raw, samples_total)
        sample_low = samples_now.astype(jnp.bfloat16)
        share_width = samples_now.shape[1] // lax.axis_size("bld")
        sample_out = lax.dynamic_slice_in_dim(
            samples_now, lax.axis_index("bld") * share_width, share_width, 1
        )
        mixed = jnp.einsum("ri,kij->krj", sample_low, tensor, preferred_element_type=jnp.float32)
        build_terms = jnp.sum(hourly[:, :, None] * mixed, axis=0)
        build_rhs = lax.psum(build_terms, "smp")
        unscaled = solve_rows(gram_sample * hour_gram(hourly), build_rhs)
        gram_raw = lax.psum(self_gram(unscaled), "bld")
        building_now, gram_build = finish(unscaled, gram_raw, buildings_total)
        build_low = building_now.astype(jnp.bfloat16)
        share_width = building_now.shape[1] // lax.axis_size("smp")
        building_out = lax.dynamic_slice_in_dim(
            building_now, lax.axis_index("smp") * share_width, share_width, 1
        )
        partial_value = jnp.einsum(
            "rj,kij->kri", build_low, tensor, preferred_element_type=jnp.float32
        )
        hour_terms = jnp.sum(sample_low.astype(jnp.float32)[None, :, :] * partial_value, axis=2)
        hour_rhs = lax.psum(hour_terms, ("smp", "bld"))
        hourly = solve_rows(gram_sample * gram_build, hour_rhs.T).T
    return (sample_out, building_out, hourly * scale_up)


def solution(mesh):
    in_specs = (P(None, "smp", "bld"), P(None, "bld"), P())
    out_specs = (P(None, ("smp", "bld")), P(None, ("bld", "smp")), P())
    return jax.shard_map(local, mesh=mesh, in_specs=in_specs, out_specs=out_specs, check_vma=False)
```

profile of v0, /device:TPU:1, one launch (start us, length us, event | category | flops | bytes accessed | tf_op | source)
XLA Modules:
  0.0 2094.5 jit_solution(17855161390660669668)
XLA Ops:
  15.2 65.3 %psum.182 = f32[64,64]{0,1:T(8,128)S(1)} all-reduce(f32[64,64]{0,1:T(8,128)S(1)} %fusion.159), channel_id=1, replica_groups=mesh['smp'=8,'bld'=16] {'bld'}, use_global_device_ids=true, to_apply=%region_0.0 | all-reduce | flops 4096 | bytes 32768 | tf_op jit(solution)/shard_map/psum | solution.py:46
  95.0 60.6 %all-reduce.11.cloned.1.call-done = f32[64,1024]{1,0:T(8,128)} async-done(((f32[64,1024]{1,0:T(8,128)}), f32[64,1024]{1,0:T(8,128)}) %all-reduce.11.cloned.1.call-update) | async-done | bytes 262160 | tf_op jit(solution)/shard_map/psum | solution.py:53
  157.7 26.2 %psum.184 = f32[64,64]{0,1:T(8,128)S(1)} all-reduce(f32[64,64]{0,1:T(8,128)S(1)} %fusion.160), channel_id=1, replica_groups=mesh['smp'=8,'bld'=16] {'smp'}, use_global_device_ids=true, to_apply=%region_6.10 | all-reduce | flops 4096 | bytes 32768 | tf_op jit(solution)/shard_map/psum | solution.py:55
  205.1 65.8 %all-reduce.13.cloned.1.call-done = f32[64,1024]{1,0:T(8,128)} async-done(((f32[64,1024]{1,0:T(8,128)}), f32[64,1024]{1,0:T(8,128)}) %all-reduce.13.cloned.1.call-update) | async-done | bytes 262160 | tf_op jit(solution)/shard_map/psum | solution.py:64
  273.0 65.3 %psum.186 = f32[64,64]{0,1:T(8,128)S(1)} all-reduce(f32[64,64]{0,1:T(8,128)S(1)} %fusion.161), channel_id=1, replica_groups=mesh['smp'=8,'bld'=16] {'bld'}, use_global_device_ids=true, to_apply=%region_10.14 | all-reduce | flops 4096 | bytes 32768 | tf_op jit(solution)/shard_map/psum | solution.py:66
  359.6 67.3 %psum.187 = f32[64,4]{0,1:T(4,128)S(1)} all-reduce(f32[64,4]{0,1:T(4,128)S(1)} %bitcast.367), channel_id=1, replica_groups=mesh['smp'=8,'bld'=16] {'smp','bld'}, use_global_device_ids=true, to_apply=%region_13.17 | all-reduce | flops 256 | bytes 2048 | tf_op jit(solution)/shard_map/psum | solution.py:77
  442.7 127.8 %all-reduce.15.cloned.1.call-done = f32[64,1024]{1,0:T(8,128)} async-done(((f32[64,1024]{1,0:T(8,128)}), f32[64,1024]{1,0:T(8,128)}) %all-reduce.15.cloned.1.call-update) | async-done | bytes 262160 | tf_op jit(solution)/shard_map/psum | solution.py:53
  572.6 26.5 %psum.189 = f32[64,64]{0,1:T(8,128)S(1)} all-reduce(f32[64,64]{0,1:T(8,128)S(1)} %fusion.162), channel_id=1, replica_groups=mesh['smp'=8,'bld'=16] {'smp'}, use_global_device_ids=true, to_apply=%region_17.23 | all-reduce | flops 4096 | bytes 32768 | tf_op jit(solution)/shard_map/psum | solution.py:55
  620.2 65.8 %all-reduce.17.cloned.1.call-done = f32[64,1024]{1,0:T(8,128)} async-done(((f32[64,1024]{1,0:T(8,128)}), f32[64,1024]{1,0:T(8,128)}) %all-reduce.17.cloned.1.call-update) | async-done | bytes 262160 | tf_op jit(solution)/shard_map/psum | solution.py:64
  688.1 64.7 %psum.191 = f32[64,64]{0,1:T(8,128)S(1)} all-reduce(f32[64,64]{0,1:T(8,128)S(1)} %fusion.163), channel_id=1, replica_groups=mesh['smp'=8,'bld'=16] {'bld'}, use_global_device_ids=true, to_apply=%region_21.27 | all-reduce | flops 4096 | bytes 32768 | tf_op jit(solution)/shard_map/psum | solution.py:66
  774.2 67.5 %psum.192 = f32[64,4]{0,1:T(4,128)S(1)} all-reduce(f32[64,4]{0,1:T(4,128)S(1)} %bitcast.368), channel_id=1, replica_groups=mesh['smp'=8,'bld'=16] {'smp','bld'}, use_global_device_ids=true, to_apply=%region_24.30 | all-reduce | flops 256 | bytes 2048 | tf_op jit(solution)/shard_map/psum | solution.py:77
  857.5 127.8 %all-reduce.19.cloned.1.call-done = f32[64,1024]{1,0:T(8,128)} async-done(((f32[64,1024]{1,0:T(8,128)}), f32[64,1024]{1,0:T(8,128)}) %all-reduce.19.cloned.1.call-update) | async-done | bytes 262160 | tf_op jit(solution)/shard_map/psum | solution.py:53
  1034.7 65.8 %all-reduce.21.cloned.1.call-done = f32[64,1024]{1,0:T(8,128)} async-done(((f32[64,1024]{1,0:T(8,128)}), f32[64,1024]{1,0:T(8,128)}) %all-reduce.21.cloned.1.call-update) | async-done | bytes 262160 | tf_op jit(solution)/shard_map/psum | solution.py:64
  1102.6 65.2 %psum.196 = f32[64,64]{0,1:T(8,128)S(1)} all-reduce(f32[64,64]{0,1:T(8,128)S(1)} %fusion.165), channel_id=1, replica_groups=mesh['smp'=8,'bld'=16] {'bld'}, use_global_device_ids=true, to_apply=%region_32.38 | all-reduce | flops 4096 | bytes 32768 | tf_op jit(solution)/shard_map/psum | solution.py:66
  1189.1 67.3 %psum.197 = f32[64,4]{0,1:T(4,128)S(1)} all-reduce(f32[64,4]{0,1:T(4,128)S(1)} %bitcast.369), channel_id=1, replica_groups=mesh['smp'=8,'bld'=16] {'smp','bld'}, use_global_device_ids=true, to_apply=%region_35.41 | all-reduce | flops 256 | bytes 2048 | tf_op jit(solution)/shard_map/psum | solution.py:77
  1272.2 127.8 %all-reduce.23.cloned.1.call-done = f32[64,1024]{1,0:T(8,128)} async-done(((f32[64,1024]{1,0:T(8,128)}), f32[64,1024]{1,0:T(8,128)}) %all-reduce.23.cloned.1.call-update) | async-done | bytes 262160 | tf_op jit(solution)/shard_map/psum | solution.py:53
  1402.0 26.5 %psum.199 = f32[64,64]{0,1:T(8,128)S(1)} all-reduce(f32[64,64]{0,1:T(8,128)S(1)} %fusion.166), channel_id=1, replica_groups=mesh['smp'=8,'bld'=16] {'smp'}, use_global_device_ids=true, to_apply=%region_39.45 | all-reduce | flops 4096 | bytes 32768 | tf_op jit(solution)/shard_map/psum | solution.py:55
  1449.7 65.8 %all-reduce.25.cloned.1.call-done = f32[64,1024]{1,0:T(8,128)} async-done(((f32[64,1024]{1,0:T(8,128)}), f32[64,1024]{1,0:T(8,128)}) %all-reduce.25.cloned.1.call-update) | async-done | bytes 262160 | tf_op jit(solution)/shard_map/psum | solution.py:64
  1517.6 64.7 %psum.201 = f32[64,64]{0,1:T(8,128)S(1)} all-reduce(f32[64,64]{0,1:T(8,128)S(1)} %fusion.167), channel_id=1, replica_groups=mesh['smp'=8,'bld'=16] {'bld'}, use_global_device_ids=true, to_apply=%region_43.49 | all-reduce | flops 4096 | bytes 32768 | tf_op jit(solution)/shard_map/psum | solution.py:66
  1603.6 67.5 %psum.202 = f32[64,4]{0,1:T(4,128)S(1)} all-reduce(f32[64,4]{0,1:T(4,128)S(1)} %bitcast.370), channel_id=1, replica_groups=mesh['smp'=8,'bld'=16] {'smp','bld'}, use_global_device_ids=true, to_apply=%region_46.52 | all-reduce | flops 256 | bytes 2048 | tf_op jit(solution)/shard_map/psum | solution.py:77
  1686.9 127.8 %all-reduce.27.cloned.1.call-done = f32[64,1024]{1,0:T(8,128)} async-done(((f32[64,1024]{1,0:T(8,128)}), f32[64,1024]{1,0:T(8,128)}) %all-reduce.27.cloned.1.call-update) | async-done | bytes 262160 | tf_op jit(solution)/shard_map/psum | solution.py:53
  1864.7 65.3 %all-reduce.29.cloned.1.call-done = f32[64,1024]{1,0:T(8,128)} async-done(((f32[64,1024]{1,0:T(8,128)}), f32[64,1024]{1,0:T(8,128)}) %all-reduce.29.cloned.1.call-update) | async-done | bytes 262160 | tf_op jit(solution)/shard_map/psum | solution.py:64
  1932.1 65.0 %psum.206 = f32[64,64]{0,1:T(8,128)S(1)} all-reduce(f32[64,64]{0,1:T(8,128)S(1)} %fusion.169), channel_id=1, replica_groups=mesh['smp'=8,'bld'=16] {'bld'}, use_global_device_ids=true, to_apply=%region_54.60 | all-reduce | flops 4096 | bytes 32768 | tf_op jit(solution)/shard_map/psum | solution.py:66
  2018.5 67.3 %psum.207 = f32[64,4]{0,1:T(4,128)S(1)} all-reduce(f32[64,4]{0,1:T(4,128)S(1)} %fusion.11), channel_id=1, replica_groups=mesh['smp'=8,'bld'=16] {'smp','bld'}, use_global_device_ids=true, to_apply=%region_57.63 | all-reduce | flops 256 | bytes 2048 | tf_op jit(solution)/shard_map/psum | solution.py:77
  (277 shorter events, 362.7 us)
Async XLA Ops:
  7.2 73.3 %copy-start.1 = (f32[4,64]{1,0:T(4,128)S(1)}, f32[4,64]{1,0:T(4,128)}, u32[]{:S(2)}) copy-start(f32[4,64]{1,0:T(4,128)} %param.14) | copy-start | bytes 3076
  7.2 7.6 copy-start
  7.2 148.4 %all-reduce.11.cloned.1.call-start = ((), (), s32[]{:S(2)}) async-start(), calls=%async_computation | async-start | bytes 524288 | tf_op jit(solution)/shard_map/psum | solution.py:53
  14.7 256.2 %all-reduce.13.cloned.1.call-start = ((), (), s32[]{:S(2)}) async-start(), calls=%async_computation.1 | async-start | bytes 524288 | tf_op jit(solution)/shard_map/psum | solution.py:64
  199.4 371.1 %all-reduce.15.cloned.1.call-start = ((), (), s32[]{:S(2)}) async-start(), calls=%async_computation.2 | async-start | bytes 524288 | tf_op jit(solution)/shard_map/psum | solution.py:53
  436.5 249.5 %all-reduce.17.cloned.1.call-start = ((), (), s32[]{:S(2)}) async-start(), calls=%async_computation.3 | async-start | bytes 524288 | tf_op jit(solution)/shard_map/psum | solution.py:64
  614.5 370.8 %all-reduce.19.cloned.1.call-start = ((), (), s32[]{:S(2)}) async-start(), calls=%async_computation.4 | async-start | bytes 524288 | tf_op jit(solution)/shard_map/psum | solution.py:53
  851.2 249.2 %all-reduce.21.cloned.1.call-start = ((), (), s32[]{:S(2)}) async-start(), calls=%async_computation.5 | async-start | bytes 524288 | tf_op jit(solution)/shard_map/psum | solution.py:64
  1029.0 371.0 %all-reduce.23.cloned.1.call-start = ((), (), s32[]{:S(2)}) async-start(), calls=%async_computation.6 | async-start | bytes 524288 | tf_op jit(solution)/shard_map/psum | solution.py:53
  1265.9 249.5 %all-reduce.25.cloned.1.call-start = ((), (), s32[]{:S(2)}) async-start(), calls=%async_computation.7 | async-start | bytes 524288 | tf_op jit(solution)/shard_map/psum | solution.py:64
  1443.9 370.8 %all-reduce.27.cloned.1.call-start = ((), (), s32[]{:S(2)}) async-start(), calls=%async_computation.8 | async-start | bytes 524288 | tf_op jit(solution)/shard_map/psum | solution.py:53
  1680.7 249.3 %all-reduce.29.cloned.1.call-start = ((), (), s32[]{:S(2)}) async-start(), calls=%async_computation.9 | async-start | bytes 524288 | tf_op jit(solution)/shard_map/psum | solution.py:64
Sparse Core Ops, SparseCore 0:
  14.8 140.7 all-reduce.10
  199.5 71.3 all-reduce.12
  436.6 133.8 all-reduce.14
  614.6 71.3 all-reduce.16
  851.4 133.8 all-reduce.18
  1029.1 71.3 all-reduce.20
  1266.0 133.8 all-reduce.22
  1444.1 71.3 all-reduce.24
  1680.8 133.8 all-reduce.26
  1858.6 71.3 all-reduce.28
where the time goes:
time: 2100 us; the launch traced here: 2090 us
  waiting for transfers between devices  900 us (43%)
  blocking collectives  859 us (41%)
  other arithmetic  196 us (9%)
  matrix products  90.9 us (4%)
  between operations  25.1 us (1%)
  local copies, waits for them, and re-layouts  22.6 us (1%)
    psum x5, waiting for transfers between devices, local(): sample_rhs = lax.psum(sample_terms, 'bld')  572 us
    psum x5, blocking collectives, local(): hour_rhs = lax.psum(hour_terms, ('smp', 'bld'))  337 us
    psum x5, waiting for transfers between devices, local(): build_rhs = lax.psum(build_terms, 'smp')  328 us
    psum x5, blocking collectives, local(): gram_raw = lax.psum(self_gram(unscaled), 'bld')  325 us
    psum x5, blocking collectives, local(): gram_raw = lax.psum(self_gram(unscaled), 'smp')  132 us
    another operation x45, other arithmetic, solve_rows(): lower_factor = jnp.linalg.cholesky(regularized(gram))  97.7 us
    another operation x30, other arithmetic, solve_rows(): lax.linalg.triangular_solve(lower_factor, middle, left_side=True, lower=T...  83.3 us
    psum x1, blocking collectives, local(): gram_build = lax.psum(self_gram(building_factor), 'bld')  65.3 us
  transfers between devices with their start and end apart: 10, of which 10 were waited for; matrix products, arithmetic and copies ran while one was open for 3% of the time, Pallas kernels for 0%

commit v1 on v0

--- a/solution.py
+++ b/solution.py
@@ -74,7 +74,8 @@
             "rj,kij->kri", build_low, tensor, preferred_element_type=jnp.float32
         )
         hour_terms = jnp.sum(sample_low.astype(jnp.float32)[None, :, :] * partial_value, axis=2)
-        hour_rhs = lax.psum(hour_terms, ("smp", "bld"))
+        reply = lax.all_gather(hour_terms, axis_name=("smp", "bld"))
+        hour_rhs = jnp.sum(reply, 0)
         hourly = solve_rows(gram_sample * gram_build, hour_rhs.T).T
     return (sample_out, building_out, hourly * scale_up)
 

time: 2100 us -> 2650 us (1.26)
  blocking collectives: 859 us -> 1410 us
    all_gather x0 -> x5, blocking collectives: none -> 883 us  [local(): reply = lax.all_gather(hour_terms, axis_name=('smp', 'bld'))]
    psum x5 -> x0, blocking collectives: 337 us -> none  [local(): hour_rhs = lax.psum(hour_terms, ('smp', 'bld'))]
where the time goes in v1:
time: 2650 us; the launch traced here: 2640 us
  blocking collectives  1410 us (53%)
  waiting for transfers between devices  899 us (34%)
  other arithmetic  197 us (7%)
  matrix products  90.9 us (3%)
    all_gather x5, blocking collectives, local(): reply = lax.all_gather(hour_terms, axis_name=('smp', 'bld'))  883 us
    psum x5, waiting for transfers between devices, local(): sample_rhs = lax.psum(sample_terms, 'bld')  571 us
    psum x5, waiting for transfers between devices, local(): build_rhs = lax.psum(build_terms, 'smp')  328 us
    psum x5, blocking collectives, local(): gram_raw = lax.psum(self_gram(unscaled), 'bld')  324 us
    psum x5, blocking collectives, local(): gram_raw = lax.psum(self_gram(unscaled), 'smp')  132 us
    another operation x45, other arithmetic, solve_rows(): lower_factor = jnp.linalg.cholesky(regularized(gram))  97.7 us
    another operation x30, other arithmetic, solve_rows(): lax.linalg.triangular_solve(lower_factor, middle, left_side=True, lower=T...  83.3 us
    psum x1, blocking collectives, local(): gram_build = lax.psum(self_gram(building_factor), 'bld')  65.3 us
  transfers between devices with their start and end apart: 10, of which 10 were waited for; matrix products, arithmetic and copies ran while one was open for 3% of the time, Pallas kernels for 0%

profile of v1, /device:TPU:1, one launch (start us, length us, event | category | flops | bytes accessed | tf_op | source)
XLA Modules:
  0.0 2640.6 jit_solution(9617583012744075826)
XLA Ops:
  15.2 65.3 %psum.147 = f32[64,64]{0,1:T(8,128)S(1)} all-reduce(f32[64,64]{0,1:T(8,128)S(1)} %fusion.164), channel_id=1, replica_groups=mesh['smp'=8,'bld'=16] {'bld'}, use_global_device_ids=true, to_apply=%region_0.0 | all-reduce | flops 4096 | bytes 32768 | tf_op jit(solution)/shard_map/psum | solution.py:46
  95.0 60.6 %all-reduce.11.cloned.1.call-done = f32[64,1024]{1,0:T(8,128)} async-done(((f32[64,1024]{1,0:T(8,128)}), f32[64,1024]{1,0:T(8,128)}) %all-reduce.11.cloned.1.call-update) | async-done | bytes 262160 | tf_op jit(solution)/shard_map/psum | solution.py:53
  205.1 65.8 %all-reduce.13.cloned.1.call-done = f32[64,1024]{1,0:T(8,128)} async-done(((f32[64,1024]{1,0:T(8,128)}), f32[64,1024]{1,0:T(8,128)}) %all-reduce.13.cloned.1.call-update) | async-done | bytes 262160 | tf_op jit(solution)/shard_map/psum | solution.py:64
  273.0 64.9 %psum.151 = f32[64,64]{0,1:T(8,128)S(1)} all-reduce(f32[64,64]{0,1:T(8,128)S(1)} %fusion.166), channel_id=1, replica_groups=mesh['smp'=8,'bld'=16] {'bld'}, use_global_device_ids=true, to_apply=%region_10.14 | all-reduce | flops 4096 | bytes 32768 | tf_op jit(solution)/shard_map/psum | solution.py:66
  345.0 176.6 %all-gather.5 = f32[128,4,64]{2,1,0:T(4,128)S(1)} all-gather(f32[1,4,64]{2,1,0:T(4,128)S(1)} %bitcast.381), channel_id=2, replica_groups=mesh['smp'=8,'bld'=16] {'smp','bld'}, dimensions={0}, use_global_device_ids=true | all-gather | bytes 132096 | tf_op jit(solution)/shard_map/all_gather | solution.py:77
  551.8 127.6 %all-reduce.15.cloned.1.call-done = f32[64,1024]{1,0:T(8,128)} async-done(((f32[64,1024]{1,0:T(8,128)}), f32[64,1024]{1,0:T(8,128)}) %all-reduce.15.cloned.1.call-update) | async-done | bytes 262160 | tf_op jit(solution)/shard_map/psum | solution.py:53
  681.5 26.5 %psum.153 = f32[64,64]{0,1:T(8,128)S(1)} all-reduce(f32[64,64]{0,1:T(8,128)S(1)} %fusion.167), channel_id=1, replica_groups=mesh['smp'=8,'bld'=16] {'smp'}, use_global_device_ids=true, to_apply=%region_17.23 | all-reduce | flops 4096 | bytes 32768 | tf_op jit(solution)/shard_map/psum | solution.py:55
  729.1 65.7 %all-reduce.17.cloned.1.call-done = f32[64,1024]{1,0:T(8,128)} async-done(((f32[64,1024]{1,0:T(8,128)}), f32[64,1024]{1,0:T(8,128)}) %all-reduce.17.cloned.1.call-update) | async-done | bytes 262160 | tf_op jit(solution)/shard_map/psum | solution.py:64
  797.0 64.7 %psum.155 = f32[64,64]{0,1:T(8,128)S(1)} all-reduce(f32[64,64]{0,1:T(8,128)S(1)} %fusion.168), channel_id=1, replica_groups=mesh['smp'=8,'bld'=16] {'bld'}, use_global_device_ids=true, to_apply=%region_21.27 | all-reduce | flops 4096 | bytes 32768 | tf_op jit(solution)/shard_map/psum | solution.py:66
  868.8 177.0 %all-gather.6 = f32[128,4,64]{2,1,0:T(4,128)S(1)} all-gather(f32[1,4,64]{2,1,0:T(4,128)S(1)} %bitcast.382), channel_id=3, replica_groups=mesh['smp'=8,'bld'=16] {'smp','bld'}, dimensions={0}, use_global_device_ids=true | all-gather | bytes 132096 | tf_op jit(solution)/shard_map/all_gather | solution.py:77
  1075.9 127.6 %all-reduce.19.cloned.1.call-done = f32[64,1024]{1,0:T(8,128)} async-done(((f32[64,1024]{1,0:T(8,128)}), f32[64,1024]{1,0:T(8,128)}) %all-reduce.19.cloned.1.call-update) | async-done | bytes 262160 | tf_op jit(solution)/shard_map/psum | solution.py:53
  1205.6 26.5 %psum.157 = f32[64,64]{0,1:T(8,128)S(1)} all-reduce(f32[64,64]{0,1:T(8,128)S(1)} %fusion.169), channel_id=1, replica_groups=mesh['smp'=8,'bld'=16] {'smp'}, use_global_device_ids=true, to_apply=%region_28.34 | all-reduce | flops 4096 | bytes 32768 | tf_op jit(solution)/shard_map/psum | solution.py:55
  1253.3 65.4 %all-reduce.21.cloned.1.call-done = f32[64,1024]{1,0:T(8,128)} async-done(((f32[64,1024]{1,0:T(8,128)}), f32[64,1024]{1,0:T(8,128)}) %all-reduce.21.cloned.1.call-update) | async-done | bytes 262160 | tf_op jit(solution)/shard_map/psum | solution.py:64
  1320.8 64.9 %psum.159 = f32[64,64]{0,1:T(8,128)S(1)} all-reduce(f32[64,64]{0,1:T(8,128)S(1)} %fusion.170), channel_id=1, replica_groups=mesh['smp'=8,'bld'=16] {'bld'}, use_global_device_ids=true, to_apply=%region_32.38 | all-reduce | flops 4096 | bytes 32768 | tf_op jit(solution)/shard_map/psum | solution.py:66
  1392.8 176.6 %all-gather.7 = f32[128,4,64]{2,1,0:T(4,128)S(1)} all-gather(f32[1,4,64]{2,1,0:T(4,128)S(1)} %bitcast.383), channel_id=4, replica_groups=mesh['smp'=8,'bld'=16] {'smp','bld'}, dimensions={0}, use_global_device_ids=true | all-gather | bytes 132096 | tf_op jit(solution)/shard_map/all_gather | solution.py:77
  1599.6 127.6 %all-reduce.23.cloned.1.call-done = f32[64,1024]{1,0:T(8,128)} async-done(((f32[64,1024]{1,0:T(8,128)}), f32[64,1024]{1,0:T(8,128)}) %all-reduce.23.cloned.1.call-update) | async-done | bytes 262160 | tf_op jit(solution)/shard_map/psum | solution.py:53
  1729.3 26.5 %psum.161 = f32[64,64]{0,1:T(8,128)S(1)} all-reduce(f32[64,64]{0,1:T(8,128)S(1)} %fusion.171), channel_id=1, replica_groups=mesh['smp'=8,'bld'=16] {'smp'}, use_global_device_ids=true, to_apply=%region_39.45 | all-reduce | flops 4096 | bytes 32768 | tf_op jit(solution)/shard_map/psum | solution.py:55
  1776.9 65.8 %all-reduce.25.cloned.1.call-done = f32[64,1024]{1,0:T(8,128)} async-done(((f32[64,1024]{1,0:T(8,128)}), f32[64,1024]{1,0:T(8,128)}) %all-reduce.25.cloned.1.call-update) | async-done | bytes 262160 | tf_op jit(solution)/shard_map/psum | solution.py:64
  1844.8 64.7 %psum.163 = f32[64,64]{0,1:T(8,128)S(1)} all-reduce(f32[64,64]{0,1:T(8,128)S(1)} %fusion.172), channel_id=1, replica_groups=mesh['smp'=8,'bld'=16] {'bld'}, use_global_device_ids=true, to_apply=%region_43.49 | all-reduce | flops 4096 | bytes 32768 | tf_op jit(solution)/shard_map/psum | solution.py:66
  1916.6 176.8 %all-gather.8 = f32[128,4,64]{2,1,0:T(4,128)S(1)} all-gather(f32[1,4,64]{2,1,0:T(4,128)S(1)} %bitcast.384), channel_id=5, replica_groups=mesh['smp'=8,'bld'=16] {'smp','bld'}, dimensions={0}, use_global_device_ids=true | all-gather | bytes 132096 | tf_op jit(solution)/shard_map/all_gather | solution.py:77
  2123.6 127.6 %all-reduce.27.cloned.1.call-done = f32[64,1024]{1,0:T(8,128)} async-done(((f32[64,1024]{1,0:T(8,128)}), f32[64,1024]{1,0:T(8,128)}) %all-reduce.27.cloned.1.call-update) | async-done | bytes 262160 | tf_op jit(solution)/shard_map/psum | solution.py:53
  2301.3 65.2 %all-reduce.29.cloned.1.call-done = f32[64,1024]{1,0:T(8,128)} async-done(((f32[64,1024]{1,0:T(8,128)}), f32[64,1024]{1,0:T(8,128)}) %all-reduce.29.cloned.1.call-update) | async-done | bytes 262160 | tf_op jit(solution)/shard_map/psum | solution.py:64
  2368.6 65.0 %psum.167 = f32[64,64]{0,1:T(8,128)S(1)} all-reduce(f32[64,64]{0,1:T(8,128)S(1)} %fusion.174), channel_id=1, replica_groups=mesh['smp'=8,'bld'=16] {'bld'}, use_global_device_ids=true, to_apply=%region_54.60 | all-reduce | flops 4096 | bytes 32768 | tf_op jit(solution)/shard_map/psum | solution.py:66
  2440.8 176.6 %all-gather.9 = f32[128,4,64]{2,1,0:T(4,128)S(1)} all-gather(f32[1,4,64]{2,1,0:T(4,128)S(1)} %bitcast.380), channel_id=6, replica_groups=mesh['smp'=8,'bld'=16] {'smp','bld'}, dimensions={0}, use_global_device_ids=true | all-gather | bytes 132096 | tf_op jit(solution)/shard_map/all_gather | solution.py:77
  (282 shorter events, 363.5 us)
Async XLA Ops:
  7.2 73.3 %copy-start.1 = (f32[4,64]{1,0:T(4,128)S(1)}, f32[4,64]{1,0:T(4,128)}, u32[]{:S(2)}) copy-start(f32[4,64]{1,0:T(4,128)} %param.14) | copy-start | bytes 3076
  7.2 7.6 copy-start
  7.2 148.4 %all-reduce.11.cloned.1.call-start = ((), (), s32[]{:S(2)}) async-start(), calls=%async_computation | async-start | bytes 524288 | tf_op jit(solution)/shard_map/psum | solution.py:53
  14.7 256.2 %all-reduce.13.cloned.1.call-start = ((), (), s32[]{:S(2)}) async-start(), calls=%async_computation.1 | async-start | bytes 524288 | tf_op jit(solution)/shard_map/psum | solution.py:64
  199.4 480.0 %all-reduce.15.cloned.1.call-start = ((), (), s32[]{:S(2)}) async-start(), calls=%async_computation.2 | async-start | bytes 524288 | tf_op jit(solution)/shard_map/psum | solution.py:53
  545.5 249.4 %all-reduce.17.cloned.1.call-start = ((), (), s32[]{:S(2)}) async-start(), calls=%async_computation.3 | async-start | bytes 524288 | tf_op jit(solution)/shard_map/psum | solution.py:64
  723.4 480.1 %all-reduce.19.cloned.1.call-start = ((), (), s32[]{:S(2)}) async-start(), calls=%async_computation.4 | async-start | bytes 524288 | tf_op jit(solution)/shard_map/psum | solution.py:53
  1069.7 249.0 %all-reduce.21.cloned.1.call-start = ((), (), s32[]{:S(2)}) async-start(), calls=%async_computation.5 | async-start | bytes 524288 | tf_op jit(solution)/shard_map/psum | solution.py:64
  1247.6 479.6 %all-reduce.23.cloned.1.call-start = ((), (), s32[]{:S(2)}) async-start(), calls=%async_computation.6 | async-start | bytes 524288 | tf_op jit(solution)/shard_map/psum | solution.py:53
  1593.3 249.4 %all-reduce.25.cloned.1.call-start = ((), (), s32[]{:S(2)}) async-start(), calls=%async_computation.7 | async-start | bytes 524288 | tf_op jit(solution)/shard_map/psum | solution.py:64
  1771.2 480.0 %all-reduce.27.cloned.1.call-start = ((), (), s32[]{:S(2)}) async-start(), calls=%async_computation.8 | async-start | bytes 524288 | tf_op jit(solution)/shard_map/psum | solution.py:53
  2117.4 249.1 %all-reduce.29.cloned.1.call-start = ((), (), s32[]{:S(2)}) async-start(), calls=%async_computation.9 | async-start | bytes 524288 | tf_op jit(solution)/shard_map/psum | solution.py:64
Sparse Core Ops, SparseCore 0:
  14.8 140.7 all-reduce.10
  199.5 71.3 all-reduce.12
  545.6 133.6 all-reduce.14
  723.5 71.2 all-reduce.16
  1069.8 133.6 all-reduce.18
  1247.7 70.9 all-reduce.20
  1593.5 133.6 all-reduce.22
  1771.3 71.3 all-reduce.24
  2117.5 133.6 all-reduce.26
  2295.1 71.3 all-reduce.28
